TPU v7x, 32 devices: a whole 2x2x4 slice. The times are simulated.
32 devices in a mesh: slices: 2 (over y), gx: 4 (over z), gy: 2 (over x), gz: 2 (over core).
Axes of the slice: x: 2, y: 2, z: 4, core: 2. Of those that a mesh axis runs over, the one named last changes fastest.
Arguments:
- gauge_links: float32 [3, 2, 3, 3, 24, 48, 128], P(None, None, None, None, ('slices', 'gx'), ('gy', 'gz')), parts along dimension 4, may hold values from -1.8 to 2.8
Outputs:
- rotated_links: float32 [3, 2, 3, 3, 24, 48, 128], P(None, None, None, None, ('slices', 'gx'), ('gy', 'gz')), parts along dimension 4
There are 2 independent parts, one for each index of `slices`. A program takes and returns all parts, laid end to end along the dimension named above; each array names one. Nothing has to cross between parts.
All inputs are finite; a program needn't handle non-finite values.
Results may differ from a plain program's by a relative error of at most 0.000084.
Values sent between devices are 32-bit elements; how exact they have to be, the bound alone decides.
A program may use at most 128 MiB of HBM per device.

v0:
```python
import functools
import math

import jax
import jax.numpy as jnp
import numpy as np
from jax import lax
from jax.experimental import pallas as pl
from jax.experimental.pallas import tpu as pltpu
from jax.sharding import PartitionSpec as P

SMEAR_RHO = 0.1
HALF_STEP = -0.04
MESH = pl.DeviceIdType.MESH
HIGHEST = lax.Precision.HIGHEST
VMEM = pl.BlockSpec(memory_space=pltpu.VMEM)
ANY = pl.BlockSpec(memory_space=pl.ANY)


def laplace_factor(freq_x, freq_y, freq_z, count_x, count_y, count_z):
    sine_x = jnp.sin(math.pi * freq_x / count_x)
    sine_y = jnp.sin(math.pi * freq_y / count_y)
    sine_z = jnp.sin(math.pi * freq_z / count_z)
    squared = (
        4.0 * (sine_x * sine_x)[:, None, None]
        + 4.0 * (sine_y * sine_y)[None, :, None]
        + 4.0 * (sine_z * sine_z)[None, None, :]
    )
    positive = squared > 0.0
    return jnp.where(positive, 12.0 / jnp.where(positive, squared, 1.0), 0.0)


def dft_tables(length):
    positions = jnp.arange(length, dtype=jnp.int32)
    phases = positions[:, None] * positions[None, :] % length
    angles = phases.astype(jnp.float32) * (2.0 * math.pi / length)
    return (jnp.cos(angles), jnp.sin(angles))


def transform(spectrum, axis_pos, direction_sign):
    length = spectrum.shape[axis_pos]
    cosine_table, sine_table = dft_tables(length)
    highest = lax.Precision.HIGHEST
    real_part = jnp.moveaxis(spectrum[0], axis_pos - 1, -1)
    imag_part = jnp.moveaxis(spectrum[1], axis_pos - 1, -1)
    out_real = jnp.dot(real_part, cosine_table, precision=highest) + direction_sign * jnp.dot(
        imag_part, sine_table, precision=highest
    )
    out_imag = jnp.dot(imag_part, cosine_table, precision=highest) - direction_sign * jnp.dot(
        real_part, sine_table, precision=highest
    )
    return jnp.moveaxis(jnp.stack([out_real, out_imag]), -1, axis_pos)


def general_solve(payload, rows_x, rows_y, depth_z):
    spectrum = jnp.stack([payload, jnp.zeros_like(payload)])
    fields_n = spectrum.shape[1]
    spectrum = transform(spectrum, 4, 1.0)
    spectrum = lax.all_to_all(spectrum, ("gy", "gz"), split_axis=4, concat_axis=3, tiled=True)
    groups_y = lax.axis_size(("gy", "gz"))
    span_z = spectrum.shape[4]
    blocks = spectrum.reshape((2, fields_n, rows_x + 1, groups_y, rows_y + 1, span_z))
    carried = jnp.roll(blocks[:, :, :, :, rows_y], 1, axis=3)
    first_row = blocks[:, :, :, :, 0] - carried
    blocks = jnp.concatenate([first_row[:, :, :, :, None], blocks[:, :, :, :, 1:rows_y]], axis=4)
    spectrum = blocks.reshape((2, fields_n, rows_x + 1, groups_y * rows_y, span_z))
    spectrum = transform(spectrum, 3, 1.0)
    spectrum = lax.all_to_all(spectrum, "gx", split_axis=3, concat_axis=2, tiled=True)
    groups_x = lax.axis_size("gx")
    span_y = spectrum.shape[3]
    blocks = spectrum.reshape((2, fields_n, groups_x, rows_x + 1, span_y, span_z))
    carried = jnp.roll(blocks[:, :, :, rows_x], 1, axis=2)
    first_row = blocks[:, :, :, 0] - carried
    blocks = jnp.concatenate([first_row[:, :, :, None], blocks[:, :, :, 1:rows_x]], axis=3)
    spectrum = blocks.reshape((2, fields_n, groups_x * rows_x, span_y, span_z))
    spectrum = transform(spectrum, 2, 1.0)
    length_x = groups_x * rows_x
    length_y = groups_y * rows_y
    freq_x = jnp.arange(length_x, dtype=jnp.float32)
    freq_y = (lax.axis_index("gx") * span_y + jnp.arange(span_y, dtype=jnp.int32)).astype(
        jnp.float32
    )
    freq_z = (lax.axis_index(("gy", "gz")) * span_z + jnp.arange(span_z, dtype=jnp.int32)).astype(
        jnp.float32
    )
    factor = laplace_factor(freq_x, freq_y, freq_z, length_x, length_y, depth_z) / float(
        length_x * length_y * depth_z
    )
    spectrum = spectrum * factor
    spectrum = transform(spectrum, 2, -1.0)
    blocks = spectrum.reshape((2, fields_n, groups_x, rows_x, span_y, span_z))
    following = jnp.roll(blocks[:, :, :, :1], -1, axis=2)
    spectrum = jnp.concatenate([blocks, following], axis=3).reshape(
        (2, fields_n, groups_x * (rows_x + 1), span_y, span_z)
    )
    spectrum = lax.all_to_all(spectrum, "gx", split_axis=2, concat_axis=3, tiled=True)
    spectrum = transform(spectrum, 3, -1.0)
    blocks = spectrum.reshape((2, fields_n, rows_x + 1, groups_y, rows_y, span_z))
    following = jnp.roll(blocks[:, :, :, :, :1], -1, axis=3)
    spectrum = jnp.concatenate([blocks, following], axis=4).reshape(
        (2, fields_n, rows_x + 1, groups_y * (rows_y + 1), span_z)
    )
    spectrum = lax.all_to_all(spectrum, ("gy", "gz"), split_axis=3, concat_axis=4, tiled=True)
    spectrum = transform(spectrum, 4, -1.0)
    return spectrum[0]


def cmul(a, b):
    return a[0] * b[0] - a[1] * b[1], a[0] * b[1] + a[1] * b[0]


def cadd(a, b):
    return a[0] + b[0], a[1] + b[1]


def conj(a):
    return a[0], -a[1]


def dot3(pairs):
    real = imag = None
    for a, b, flip_a, flip_b in pairs:
        rr, ii = a[0] * b[0], a[1] * b[1]
        ri, ir = a[0] * b[1], a[1] * b[0]
        r = rr - ii if flip_a == flip_b else rr + ii
        i = {(0, 0): lambda: ri + ir, (0, 1): lambda: ir - ri, (1, 0): lambda: ri - ir}[(flip_a, flip_b)]()
        real = r if real is None else real + r
        imag = i if imag is None else imag + i
    return real, imag


def mat_mul(a, b):
    return [[dot3([(a[r][m], b[m][c], 0, 0) for m in range(3)]) for c in range(3)] for r in range(3)]


def mat_mul_dag(a, b):
    return [[dot3([(a[r][m], b[c][m], 0, 1) for m in range(3)]) for c in range(3)] for r in range(3)]


def dag_mat_mul(a, b):
    return [[dot3([(a[m][r], b[m][c], 1, 0) for m in range(3)]) for c in range(3)] for r in range(3)]


def anti_parts(m):
    third = (m[0][0][1] + m[1][1][1] + m[2][2][1]) * (1.0 / 3.0)
    out = [m[0][0][1] - third, m[1][1][1] - third]
    for r, c in ((0, 1), (0, 2), (1, 2)):
        out.append(0.5 * (m[r][c][0] - m[c][r][0]))
        out.append(0.5 * (m[r][c][1] + m[c][r][1]))
    return out


def exp_parts(parts, scale):
    v = [0.5 * scale * p for p in parts]
    h0, h1 = v[0], v[1]
    h2 = -h0 - h1
    h01, h02, h12 = (v[3], -v[2]), (v[5], -v[4]), (v[7], -v[6])
    n01, n02, n12 = [h[0] * h[0] + h[1] * h[1] for h in (h01, h02, h12)]
    s0, s1, s2 = h0 * h0, h1 * h1, h2 * h2
    k00, k11, k22 = s0 + n01 + n02, s1 + n01 + n12, s2 + n02 + n12
    p02 = cmul(h01, h12)
    q = cmul(h02, conj(h12))
    w = cmul(conj(h01), h02)
    k01 = (q[0] - h2 * h01[0], q[1] - h2 * h01[1])
    k02 = (p02[0] - h1 * h02[0], p02[1] - h1 * h02[1])
    k12 = (w[0] - h0 * h12[0], w[1] - h0 * h12[1])
    t = 0.5 * (k00 + k11 + k22)
    d = h0 * h1 * h2 + 2.0 * (p02[0] * h02[0] + p02[1] * h02[1]) - h0 * n12 - h1 * n02 - h2 * n01
    t2 = t * t
    q0 = (1.0 - d * d * (1.0 / 720.0), d * (t * (1.0 / 120.0) - 1.0 / 6.0))
    q1 = (d * (1.0 / 24.0 - t * (1.0 / 360.0)), 1.0 - t * (1.0 / 6.0) + t2 * (1.0 / 120.0))
    q2 = (t * (1.0 / 24.0) - 0.5 - t2 * (1.0 / 720.0), d * (1.0 / 120.0))
    q00, q01, q02, q11, q12, q22 = cmul(q0, q0), cmul(q0, q1), cmul(q0, q2), cmul(q1, q1), cmul(q1, q2), cmul(q2, q2)
    e0 = [q00[n] + 2.0 * d * q12[n] for n in range(2)]
    e1 = [2.0 * (q01[n] + t * q12[n]) + d * q22[n] for n in range(2)]
    e2 = [2.0 * q02[n] + q11[n] + t * q22[n] for n in range(2)]
    out = [[None] * 3 for _ in range(3)]
    for r, (h, k) in enumerate(((h0, k00), (h1, k11), (h2, k22))):
        out[r][r] = (e0[0] + e1[0] * h + e2[0] * k, e0[1] + e1[1] * h + e2[1] * k)
    for r, c, h, k in ((0, 1, h01, k01), (0, 2, h02, k02), (1, 2, h12, k12)):
        out[r][c] = cadd(cmul(e1, h), cmul(e2, k))
        out[c][r] = cadd(cmul(e1, conj(h)), cmul(e2, conj(k)))
    return out


def mat_map(fn, m):
    return [[(fn(e[0]), fn(e[1])) for e in row] for row in m]


def load_mat(ref, base, x, row):
    return [
        [tuple(ref[base + 9 * part + 3 * r + c, x, row : row + 8, :] for part in range(2)) for c in range(3)]
        for r in range(3)
    ]


def forward_z(value):
    return pltpu.roll(value, value.shape[1] - 1, 1)


def backward_z(value):
    return pltpu.roll(value, 1, 1)


def staple_kernel(l_ref, hx_ref, hy_ref, gu_ref, lx_ref, ly_ref, rim_ref, ext):
    rows_x, rows_y = l_ref.shape[1], l_ref.shape[2]

    def fill(n, _):
        ext[n, 0:rows_x, 0:rows_y, :] = l_ref[n]
        return 0

    lax.fori_loop(0, 54, fill, 0)

    def fill_x(n, _):
        ext[18 + n, rows_x, 0:rows_y, :] = hx_ref[n]
        return 0

    lax.fori_loop(0, 36, fill_x, 0)
    for n in range(36):
        target = n if n < 18 else n + 18
        for x in range(rows_x):
            ext[target, x, rows_y : rows_y + 1, :] = hy_ref[x, n : n + 1, :]

    def step(x, _):
        for row in (0, rows_y - 8):
            here = slice(row, row + 8)
            acc = [None] * 3

            def add(direction, parts, sign=1.0):
                if acc[direction] is None:
                    acc[direction] = parts if sign > 0 else [-p for p in parts]
                elif sign > 0:
                    acc[direction] = [p + q for p, q in zip(acc[direction], parts)]
                else:
                    acc[direction] = [p - q for p, q in zip(acc[direction], parts)]

            for i, j in ((0, 1), (0, 2), (1, 2)):
                ui, uj = load_mat(ext, 18 * i, x, row), load_mat(ext, 18 * j, x, row)
                if j == 1:
                    ui_j = load_mat(ext, 18 * i, x, row + 1)
                else:
                    ui_j = mat_map(forward_z, ui)
                if i == 0:
                    uj_i = load_mat(ext, 18 * j, x + 1, row)
                else:
                    uj_i = load_mat(ext, 18 * j, x, row + 1)
                b = mat_mul(ui, uj_i)
                a = mat_mul(uj, ui_j)
                plaquette = anti_parts(mat_mul_dag(a, b))
                add(i, plaquette)
                add(j, plaquette, -1.0)
                low_i = anti_parts(mat_mul_dag(dag_mat_mul(uj, b), ui_j))
                low_j = anti_parts(mat_mul_dag(dag_mat_mul(ui, a), uj_i))
                if j == 2:
                    add(i, [backward_z(p) for p in low_i])
                for parts, shift, slot in ((low_i, j, 0), (low_j, i, 0 if j == 1 else 8)):
                    for n, p in enumerate(parts):
                        if shift == 0:
                            lx_ref[slot + n, x, here, :] = p
                        elif shift == 1:
                            ly_ref[slot + n, x, row + 1 : row + 9, :] = p
                            if row:
                                rim_ref[x, slot + n : slot + n + 1, :] = p[7:8, :]
            for direction in range(3):
                for n in range(8):
                    gu_ref[8 * direction + n, x, here, :] = acc[direction][n]
        return 0

    lax.fori_loop(0, rows_x, step, 0)


def smear_kernel(fast, l_ref, gu_ref, lx_ref, ly_ref, rx_ref, ry_ref, table_ref, v_ref, s_ref, a0, a1, dz, pack):
    rows_x, rows_y = l_ref.shape[1], l_ref.shape[2]

    def step(x, _):
        before = jnp.maximum(x - 1, 0)
        for row in (0, rows_y - 8):
            here = slice(row, row + 8)
            top = lax.broadcasted_iota(jnp.int32, (8, 128), 0) == 0

            def low_x(n):
                return jnp.where(x == 0, rx_ref[n, here, :], lx_ref[n, before, here, :])

            def low_y(n):
                value = ly_ref[n, x, here, :]
                if row == 0:
                    value = jnp.where(top, ry_ref[x, n : n + 1, :], value)
                return value

            for direction in range(3):
                parts = []
                for n in range(8):
                    p = gu_ref[8 * direction + n, x, here, :]
                    if direction == 0:
                        p = p + low_y(n)
                    elif direction == 1:
                        p = p + low_x(n)
                    else:
                        p = p + low_x(8 + n) + low_y(8 + n)
                    parts.append(p)
                smeared = mat_mul(exp_parts(parts, SMEAR_RHO), load_mat(l_ref, 18 * direction, x, row))
                for r in range(3):
                    for c in range(3):
                        for part in range(2):
                            v_ref[18 * direction + 9 * part + 3 * r + c, x, here, :] = smeared[r][c][part]
                for n, p in enumerate(anti_parts(smeared)):
                    if direction == 0:
                        a0[n, x, here, :] = p
                    elif direction == 1:
                        a1[n, x, row + 1 : row + 9, :] = p
                    else:
                        dz[n, x, here, :] = p - backward_z(p)
        return 0

    lax.fori_loop(0, rows_x, step, 0)

    def divergence(n, _):
        pack[n] = jnp.zeros(pack.shape[1:], jnp.float32)
        for x in range(rows_x):
            total = a0[n, x] + dz[n, x] + a1[n, x, 1 : rows_y + 1, :]
            if x:
                total = total - a0[n, x - 1]
            lanes = slice(128 * (x // 2), 128 * (x // 2) + 128)
            pack[n, x % 2, 0:rows_y, lanes] = total
            pack[n, x % 2, 1:rows_y, lanes] = pack[n, x % 2, 1:rows_y, lanes] - a1[n, x, 1:rows_y, :]
            pack[n, x % 2, rows_y : rows_y + 1, lanes] = a1[n, x, rows_y : rows_y + 1, :]
        pack[n, 1, 0:rows_y, 128:256] = a0[n, rows_x - 1]
        return 0

    lax.fori_loop(0, 8, divergence, 0)
    if fast:
        out = jnp.dot(
            pack[...].reshape(256, 256), table_ref[...], precision=HIGHEST, preferred_element_type=jnp.float32
        )
        for half in range(2):
            s_ref[:, half] = out[:, 128 * half : 128 * half + 128].reshape(8, 2, 16, 128)
    else:
        s_ref[...] = pack[...]


def solve_kernel(r_ref, ty_ref, tyi_ref, cf_ref, ci_ref, f_ref, o_ref):
    half = lax.axis_index("gz")
    planes = []
    for gx in range(4):
        for xp in range(2):
            block = r_ref[4 * gx : 4 * gx + 4, xp].reshape(64, 128)
            planes.append(
                jnp.dot(ty_ref[...], block, precision=HIGHEST, preferred_element_type=jnp.float32)
            )
    turned = [pltpu.roll(p, 64, 1) for p in planes]
    modes = []
    for m in range(6):
        total = None
        for n in range(8):
            term = planes[n] * cf_ref[m, n, 0:1, :] + turned[n] * cf_ref[m, n, 1:2, :]
            total = term if total is None else total + term
        modes.append(total * f_ref[half, m])
    turned = [pltpu.roll(p, 64, 1) for p in modes]
    for gx in range(4):
        for xp in range(2):
            total = None
            for m in range(6):
                term = modes[m] * ci_ref[2 * gx + xp, m, 0:1, :] + turned[m] * ci_ref[2 * gx + xp, m, 1:2, :]
                total = term if total is None else total + term
            out = jnp.dot(tyi_ref[...], total, precision=HIGHEST, preferred_element_type=jnp.float32)
            o_ref[4 * gx : 4 * gx + 4, xp] = out.reshape(4, 16, 128)


def rotate_kernel(fast, q_ref, v_ref, table_ref, o_ref, acc, g):
    rows_x, rows_y = v_ref.shape[1], v_ref.shape[2]
    if fast:
        left = jnp.concatenate([q_ref[:, 0].reshape(256, 128), q_ref[:, 1].reshape(256, 128)], axis=1)
        out = jnp.dot(left, table_ref[...], precision=HIGHEST, preferred_element_type=jnp.float32)
        for part in range(2):
            acc[:, 2 * part : 2 * part + 2] = out[:, 128 * part : 128 * part + 128].reshape(8, 2, 16, 128)
        src = acc
    else:
        src = q_ref

    def exponent(x, _):
        for row in (0, 8):
            here = slice(row, row + 8)
            m = exp_parts([src[n, x, here, :] for n in range(8)], HALF_STEP)
            for r in range(3):
                for c in range(3):
                    for part in range(2):
                        g[9 * part + 3 * r + c, x, here, :] = m[r][c][part]
        return 0

    lax.fori_loop(0, rows_x + 1, exponent, 0)

    def step(x, _):
        for row in (0, rows_y - 8):
            here = slice(row, row + 8)
            centre = load_mat(g, 0, x, row)
            for direction in range(3):
                if direction == 0:
                    other = load_mat(g, 0, x + 1, row)
                elif direction == 1:
                    other = load_mat(g, 0, x, row + 1)
                else:
                    other = mat_map(forward_z, centre)
                out = mat_mul_dag(mat_mul(centre, load_mat(v_ref, 18 * direction, x, row)), other)
                for r in range(3):
                    for c in range(3):
                        for part in range(2):
                            o_ref[18 * direction + 9 * part + 3 * r + c, x, here, :] = out[r][c][part]
        return 0

    lax.fori_loop(0, rows_x, step, 0)


def neighbour(axis_sizes, step_x, step_y):
    n_x, n_y, n_z = axis_sizes
    gx = lax.axis_index("gx")
    block = lax.axis_index("gy") * n_z + lax.axis_index("gz")
    if step_x:
        return {"gx": lax.rem(gx + n_x + step_x, n_x)}
    block = lax.rem(block + n_y * n_z + step_y, n_y * n_z)
    return {"gy": lax.div(block, n_z), "gz": lax.rem(block, n_z)}


def exchange_kernel(sizes, way, pick, sx_ref, sy_ref, rx_ref, ry_ref, send, recv):
    barrier = pltpu.get_barrier_semaphore()
    for device in (neighbour(sizes, -way, 0), neighbour(sizes, 0, -way)):
        pl.semaphore_signal(barrier, inc=1, device_id=device, device_id_type=MESH)
    pl.semaphore_wait(barrier, 2)
    first, count, x = pick
    copies = []
    for n, (src, dst, device) in enumerate(
        (
            (sx_ref.at[pl.ds(first, count), x], rx_ref, neighbour(sizes, way, 0)),
            (sy_ref, ry_ref, neighbour(sizes, 0, way)),
        )
    ):
        copies.append(
            pltpu.make_async_remote_copy(
                src_ref=src,
                dst_ref=dst,
                send_sem=send.at[n],
                recv_sem=recv.at[n],
                device_id=device,
                device_id_type=MESH,
            )
        )
        copies[-1].start()
    for copy in copies:
        copy.wait()


def exchange(sizes, way, pick, key, sx, sy):
    shapes = (
        jax.ShapeDtypeStruct((pick[1],) + sx.shape[2:], jnp.float32),
        jax.ShapeDtypeStruct(sy.shape, jnp.float32),
    )
    return pl.pallas_call(
        functools.partial(exchange_kernel, sizes, way, pick),
        out_shape=shapes,
        in_specs=[ANY, ANY],
        out_specs=(ANY, ANY),
        scratch_shapes=[pltpu.SemaphoreType.DMA((2,)), pltpu.SemaphoreType.DMA((2,))],
        compiler_params=pltpu.CompilerParams(collective_id=key, has_side_effects=True),
    )(sx, sy)


def swap_kernel(sizes, s_ref, r_ref, send, recv, local):
    n_x, n_y, n_z = sizes
    total = n_x * n_y * n_z
    me = (lax.axis_index("gx") * n_y + lax.axis_index("gy")) * n_z + lax.axis_index("gz")

    def device(index):
        return {
            "gx": lax.div(index, n_y * n_z),
            "gy": lax.rem(lax.div(index, n_z), n_y),
            "gz": lax.rem(index, n_z),
        }

    barrier = pltpu.get_barrier_semaphore()
    for offset in range(1, total):
        pl.semaphore_signal(
            barrier, inc=1, device_id=device(lax.rem(me + offset, total)), device_id_type=MESH
        )
    own = pltpu.make_async_copy(s_ref.at[me], r_ref.at[me], local)
    own.start()
    pl.semaphore_wait(barrier, total - 1)
    copies = []
    for offset in sorted(range(1, total), key=lambda o: -min(o, total - o)):
        peer = lax.rem(me + offset, total)
        copies.append(
            pltpu.make_async_remote_copy(
                src_ref=s_ref.at[peer],
                dst_ref=r_ref.at[me],
                send_sem=send.at[offset],
                recv_sem=recv.at[offset],
                device_id=device(peer),
                device_id_type=MESH,
            )
        )
        copies[-1].start()
    own.wait()
    for copy in copies:
        copy.wait()


def swap(sizes, key, blocks):
    total = blocks.shape[0]
    return pl.pallas_call(
        functools.partial(swap_kernel, sizes),
        out_shape=jax.ShapeDtypeStruct(blocks.shape, jnp.float32),
        in_specs=[ANY],
        out_specs=ANY,
        scratch_shapes=[
            pltpu.SemaphoreType.DMA((total,)),
            pltpu.SemaphoreType.DMA((total,)),
            pltpu.SemaphoreType.DMA,
        ],
        compiler_params=pltpu.CompilerParams(collective_id=key, has_side_effects=True),
    )(blocks)


def real_basis(length):
    x = np.arange(length)
    freq = np.zeros(length, np.int64)
    rows = np.zeros((length, length))
    rows[0] = 1.0 / math.sqrt(length)
    for n in range(1, length):
        k = (n + 1) // 2
        freq[n] = k
        angle = 2.0 * math.pi * ((k * x) % length) / length
        if 2 * k == length:
            rows[n] = np.cos(angle) / math.sqrt(length)
        else:
            rows[n] = (np.cos(angle) if n % 2 else np.sin(angle)) * math.sqrt(2.0 / length)
    return rows, 4.0 * np.sin(math.pi * freq / length) ** 2


def tables():
    tz, pz = real_basis(128)
    ty, py = real_basis(48)
    tx, px = real_basis(12)
    wide = np.zeros((2, 128, 2, 2, 64))
    for p in range(2):
        wide[p, :, :, p, :] = tz.T.reshape(128, 2, 64)
    wide = wide.reshape(256, 256)
    fy = np.zeros((48, 4, 16))
    iy = np.zeros((4, 16, 48))
    for b in range(4):
        fy[:, b, :12] = ty[:, 12 * b : 12 * b + 12]
        fy[:, b, 12] = -ty[:, (12 * b + 12) % 48]
        for r in range(13):
            iy[b, r] = ty[:, (12 * b + r) % 48]
    cf = np.zeros((6, 8, 2, 2, 64))
    ci = np.zeros((8, 6, 2, 2, 64))
    factor = np.zeros((2, 6, 48, 2, 64))
    for m in range(6):
        for q in range(2):
            squared = px[m + 6 * q] + py[None, :, None] + pz.reshape(2, 1, 64)
            factor[:, m, :, q] = np.where(squared > 1e-9, 12.0 / np.where(squared > 1e-9, squared, 1.0), 0.0)
            for gx in range(4):
                for xp in range(2):
                    for turn in range(2):
                        x = xp + 2 * (q if turn == 0 else 1 - q)
                        kx = m + 6 * q
                        site = (3 * gx + x) % 12
                        cf[m, 2 * gx + xp, turn, q] = -tx[kx, site] if x == 3 else tx[kx, site]
                        back = m + 6 * (q if turn == 0 else 1 - q)
                        ci[2 * gx + xp, m, turn, q] = tx[back, (3 * gx + xp + 2 * q) % 12]
    flat = lambda t, shape: jnp.asarray(t.reshape(shape), jnp.float32)
    return (
        flat(wide, (256, 256)),
        flat(wide.T.copy(), (256, 256)),
        flat(fy, (48, 64)),
        flat(iy, (64, 48)),
        flat(cf, (6, 8, 2, 128)),
        flat(ci, (8, 6, 2, 128)),
        flat(factor, (2, 6, 48, 128)),
    )


def local(kernel, shapes, scratch, *operands):
    single = isinstance(shapes[0], int)
    out = pl.pallas_call(
        kernel,
        out_shape=tuple(jax.ShapeDtypeStruct(s, jnp.float32) for s in ((shapes,) if single else shapes)),
        in_specs=[VMEM] * len(operands),
        out_specs=tuple(VMEM for _ in ((shapes,) if single else shapes)),
        scratch_shapes=[pltpu.VMEM(s, jnp.float32) for s in scratch],
        compiler_params=pltpu.CompilerParams(vmem_limit_bytes=40 << 20),
    )(*operands)
    return out[0] if single else out


def shards(sizes, gauge_links):
    rows_x, rows_y, depth = gauge_links.shape[4:]
    fast = sizes == (4, 2, 2)
    wide, wide_back, fy, iy, cf, ci, factor = tables()
    links = gauge_links.reshape(54, rows_x, rows_y, depth)
    first = links[:, :, 0, :]
    edge = jnp.moveaxis(jnp.concatenate([first[:18], first[36:]], axis=0), 0, 1)
    hx, hy = exchange(sizes, -1, (18, 36, 0), 1, links, edge)
    gu, lx, ly, rim = local(
        staple_kernel,
        (
            (24, rows_x, rows_y, depth),
            (16, rows_x, rows_y, depth),
            (16, rows_x, rows_y + 1, depth),
            (rows_x, 16, depth),
        ),
        [(54, rows_x + 1, 16, depth)],
        links,
        hx,
        hy,
    )
    rx, ry = exchange(sizes, 1, (0, 16, rows_x - 1), 2, lx, rim)
    spectral = (8, 2, 2, 16, 128) if fast else (8, 2, 16, 256)
    smeared, blocks = local(
        functools.partial(smear_kernel, fast),
        ((54, rows_x, rows_y, depth), spectral),
        [
            (8, rows_x, rows_y, depth),
            (8, rows_x, rows_y + 1, depth),
            (8, rows_x, rows_y, depth),
            (8, 2, 16, 256),
        ],
        links,
        gu,
        lx,
        ly,
        rx,
        ry,
        wide,
    )
    if fast:
        received = swap(sizes, 3, blocks.reshape(16, 2, 16, 128))
        solved = local(solve_kernel, (16, 2, 16, 128), [], received, fy, iy, cf, ci, factor)
        accel = swap(sizes, 4, solved).reshape(8, 2, 2, 16, 128)
    else:
        used = blocks[:, :, : rows_y + 1]
        payload = jnp.concatenate([used[..., :depth], used[..., depth:]], axis=1)
        accel = general_solve(payload, rows_x, rows_y, depth)
        accel = jnp.pad(accel, ((0, 0), (0, 0), (0, 16 - accel.shape[2]), (0, 0)))
    rotated = local(
        functools.partial(rotate_kernel, fast),
        (54, rows_x, rows_y, depth),
        [(8, 4, 16, 128), (18, rows_x + 1, 16, depth)],
        accel,
        smeared,
        wide_back,
    )
    return rotated.reshape(gauge_links.shape)


def solution(mesh):
    sizes = (mesh.shape["gx"], mesh.shape["gy"], mesh.shape["gz"])
    return jax.shard_map(
        functools.partial(shards, sizes),
        mesh=mesh,
        in_specs=(P(None, None, None, None, ("slices", "gx"), ("gy", "gz"), None),),
        out_specs=P(None, None, None, None, ("slices", "gx"), ("gy", "gz"), None),
        check_vma=False,
    )
```

profile of v0, /device:TPU:0, one launch (start us, length us, event | category | flops | bytes accessed | tf_op | source)
XLA Modules:
  0.0 68.1 jit_solution(8721209982577641883)
XLA Ops:
  0.0 1.3 %copy.9 = f32[3,2,3,3,3,12,128]{6,5,4,3,2,1,0:T(8,128)S(1)} copy(f32[3,2,3,3,3,12,128]{6,1,5,4,3,2,0:T(2,128)} %param.8) | data formatting | bytes 1990656 | tf_op args[0]
  1.5 0.8 %copy.11.sy_ref = f32[3,36,128]{2,1,0:T(8,128)} copy(f32[3,36,128]{2,0,1:T(4,128)S(1)} %maximum_bitcast_fusion) | data formatting | bytes 110592 | tf_op jit(solution)/shard_map/transpose | solution.py:599
  2.5 10.1 %shard_map.82 = (f32[36,12,128]{2,1,0:T(8,128)}, f32[3,36,128]{2,1,0:T(8,128)}) custom-call(f32[54,3,12,128]{3,2,1,0:T(8,128)} %bitcast.13, f32[3,36,128]{2,1,0:T(8,128)} %copy.11.sy_ref), custom_call_target="tpu_custom_call" | custom-call | tf_op jit(solution)/shard_map/pallas_call | solution.py:456
  12.6 1.3 %copy-done.1 = f32[3,2,3,3,3,12,128]{6,5,4,3,2,1,0:T(8,128)S(1)} copy-done((f32[3,2,3,3,3,12,128]{6,5,4,3,2,1,0:T(8,128)S(1)}, f32[3,2,3,3,3,12,128]{6,5,4,3,2,1,0:T(8,128)}, u32[]{:S(2)}) %copy-start.1) | copy-done | bytes 995352
  13.9 1.0 %copy-done.10 = f32[36,12,128]{2,1,0:T(8,128)S(1)} copy-done((f32[36,12,128]{2,1,0:T(8,128)S(1)}, f32[36,12,128]{2,1,0:T(8,128)}, u32[]{:S(2)}) %copy-start.10) | copy-done | bytes 221208
  14.9 0.8 %copy-done.16 = f32[3,36,128]{2,1,0:T(8,128)S(1)} copy-done((f32[3,36,128]{2,1,0:T(8,128)S(1)}, f32[3,36,128]{2,1,0:T(8,128)}, u32[]{:S(2)}) %copy-start.16) | copy-done | bytes 55320
  15.7 3.9 %shard_map.83 = (f32[24,3,12,128]{3,2,1,0:T(8,128)S(1)}, f32[16,3,12,128]{3,2,1,0:T(8,128)S(1)}, f32[16,3,13,128]{3,2,1,0:T(8,128)S(1)}, f32[3,16,128]{2,1,0:T(8,128)S(1)}) custom-call(f32[54,3,12,128]{3,2,1,0:T(8,128)S(1)} %bitcast.14, f32[36,12,128]{2,1,0:T(8,128)S(1)} %copy-done.10, f32[3,36,128]{2,1,0:T(8,128)S(1)} %copy-done.16), custom_call_target="tpu_custom_call" | custom-call | tf_op jit(solution)/shard_map/pallas_call | solution.py:582
  20.4 0.7 %copy-done.8 = f32[16,3,13,128]{3,2,1,0:T(8,128)} copy-done((f32[16,3,13,128]{3,2,1,0:T(8,128)}, f32[16,3,13,128]{3,2,1,0:T(8,128)S(1)}, u32[]{:S(2)}) %copy-start.8) | copy-done | bytes 319512
  21.7 7.4 %shard_map.84 = (f32[16,12,128]{2,1,0:T(8,128)}, f32[3,16,128]{2,1,0:T(8,128)}) custom-call(f32[16,3,12,128]{3,2,1,0:T(8,128)} %copy-done.3, f32[3,16,128]{2,1,0:T(8,128)} %copy-done.21), custom_call_target="tpu_custom_call" | custom-call | tf_op jit(solution)/shard_map/pallas_call | solution.py:456
  29.1 1.0 %copy-done.4 = f32[16,3,12,128]{3,2,1,0:T(8,128)S(1)} copy-done((f32[16,3,12,128]{3,2,1,0:T(8,128)S(1)}, f32[16,3,12,128]{3,2,1,0:T(8,128)}, u32[]{:S(2)}) %copy-start.4) | copy-done | bytes 294936
  30.1 1.0 %copy-done.9 = f32[16,3,13,128]{3,2,1,0:T(8,128)S(1)} copy-done((f32[16,3,13,128]{3,2,1,0:T(8,128)S(1)}, f32[16,3,13,128]{3,2,1,0:T(8,128)}, u32[]{:S(2)}) %copy-start.9) | copy-done | bytes 319512
  31.1 0.9 %copy-done.13 = f32[256,256]{1,0:T(8,128)S(1)} copy-done((f32[256,256]{1,0:T(8,128)S(1)}, f32[256,256]{1,0:T(8,128)}, u32[]{:S(2)}) %copy-start.13) | copy-done | bytes 262168
  32.1 0.9 %copy-done.15 = f32[16,12,128]{2,1,0:T(8,128)S(1)} copy-done((f32[16,12,128]{2,1,0:T(8,128)S(1)}, f32[16,12,128]{2,1,0:T(8,128)}, u32[]{:S(2)}) %copy-start.15) | copy-done | bytes 98328
  33.7 1.8 %shard_map.85 = (f32[54,3,12,128]{3,2,1,0:T(8,128)S(1)}, f32[8,2,2,16,128]{4,3,2,1,0:T(8,128)S(1)}) custom-call(f32[54,3,12,128]{3,2,1,0:T(8,128)S(1)} %bitcast.15, f32[24,3,12,128]{3,2,1,0:T(8,128)S(1)} %get-tuple-element.17.gu_ref, f32[16,3,12,128]{3,2,1,0:T(8,128)S(1)} %copy-done.4, f32[16,3,13,128]{3,2,1,0:T(8,128)S(1)} %copy-done.9, ...), custom_call_target="tpu_custom_call" | custom-call | tf_op jit(solution)/shard_map/pallas_call | solution.py:582
  36.2 11.5 %shard_map.86.r_ref = f32[16,2,16,128]{3,2,1,0:T(8,128)} custom-call(f32[16,2,16,128]{3,2,1,0:T(8,128)} %bitcast.18), custom_call_target="tpu_custom_call" | custom-call | tf_op jit(solution)/shard_map/pallas_call | solution.py:507
  47.7 0.9 %copy-done.6 = f32[16,2,16,128]{3,2,1,0:T(8,128)S(1)} copy-done((f32[16,2,16,128]{3,2,1,0:T(8,128)S(1)}, f32[16,2,16,128]{3,2,1,0:T(8,128)}, u32[]{:S(2)}) %copy-start.6) | copy-done | bytes 262168
  48.7 0.8 %copy-done.17 = f32[8,6,2,128]{3,2,1,0:T(2,128)S(1)} copy-done((f32[8,6,2,128]{3,2,1,0:T(2,128)S(1)}, f32[8,6,2,128]{3,2,1,0:T(2,128)}, u32[]{:S(2)}) %copy-start.17) | copy-done | bytes 49176
  49.5 0.8 %copy-done.18 = f32[6,8,2,128]{3,2,1,0:T(2,128)S(1)} copy-done((f32[6,8,2,128]{3,2,1,0:T(2,128)S(1)}, f32[6,8,2,128]{3,2,1,0:T(2,128)}, u32[]{:S(2)}) %copy-start.18) | copy-done | bytes 49176
  50.3 0.8 %copy-done.19 = f32[64,48]{1,0:T(8,128)S(1)} copy-done((f32[64,48]{1,0:T(8,128)S(1)}, f32[64,48]{1,0:T(8,128)}, u32[]{:S(2)}) %copy-start.19) | copy-done | bytes 12312
  51.8 1.0 %shard_map.87.s_ref = f32[16,2,16,128]{3,2,1,0:T(8,128)S(1)} custom-call(f32[16,2,16,128]{3,2,1,0:T(8,128)S(1)} %copy-done.6, f32[48,64]{1,0:T(8,128)S(1)} %copy-done.22, f32[64,48]{1,0:T(8,128)S(1)} %copy-done.19, f32[6,8,2,128]{3,2,1,0:T(2,128)S(1)} %copy-done.18, f32[8,6,2,128]{3,2,1,0:T(2,128)S(1)} %copy-done.17, f32[2,6,48,128]{3,2,1,0:T(8,128)S(1)} %copy-done.11), custom_call_target="tpu_custom_call" | custom-call | tf_op jit(solution)/shard_map/pallas_call | solution.py:582
  53.4 10.6 %shard_map.88 = f32[16,2,16,128]{3,2,1,0:T(8,128)} custom-call(f32[16,2,16,128]{3,2,1,0:T(8,128)} %copy-done.7), custom_call_target="tpu_custom_call" | custom-call | tf_op jit(solution)/shard_map/pallas_call | solution.py:507
  64.0 0.9 %copy-done.5 = f32[16,2,16,128]{3,2,1,0:T(8,128)S(1)} copy-done((f32[16,2,16,128]{3,2,1,0:T(8,128)S(1)}, f32[16,2,16,128]{3,2,1,0:T(8,128)}, u32[]{:S(2)}) %copy-start.5) | copy-done | bytes 262168
  65.0 1.7 %shard_map.89 = f32[54,3,12,128]{3,2,1,0:T(8,128)S(1)} custom-call(f32[8,2,2,16,128]{4,3,2,1,0:T(8,128)S(1)} %bitcast.17, f32[54,3,12,128]{3,2,1,0:T(8,128)S(1)} %get-tuple-element.24.v_ref, f32[256,256]{1,0:T(8,128)S(1)} %copy-done.12), custom_call_target="tpu_custom_call" | custom-call | tf_op jit(solution)/shard_map/pallas_call | solution.py:582
  66.7 1.5 %copy.12 = f32[3,2,3,3,3,12,128]{6,1,5,4,3,2,0:T(2,128)} copy(f32[3,2,3,3,3,12,128]{6,5,4,3,2,1,0:T(8,128)S(1)} %bitcast.16) | data formatting | bytes 1990656 | tf_op jit(solution)/shard_map/reshape | solution.py:650
  (37 shorter events, 4.6 us)
Async XLA Ops:
  1.4 1.1 %copy-start = (f32[3,2,3,3,3,12,128]{6,5,4,3,2,1,0:T(8,128)}, f32[3,2,3,3,3,12,128]{6,5,4,3,2,1,0:T(8,128)S(1)}, u32[]{:S(2)}) copy-start(f32[3,2,3,3,3,12,128]{6,5,4,3,2,1,0:T(8,128)S(1)} %copy.9) | copy-start | bytes 2985988
  12.6 1.3 %copy-start.1 = (f32[3,2,3,3,3,12,128]{6,5,4,3,2,1,0:T(8,128)S(1)}, f32[3,2,3,3,3,12,128]{6,5,4,3,2,1,0:T(8,128)}, u32[]{:S(2)}) copy-start(f32[3,2,3,3,3,12,128]{6,5,4,3,2,1,0:T(8,128)} %copy-done) | copy-start | bytes 2985988
  13.9 1.0 %copy-start.10 = (f32[36,12,128]{2,1,0:T(8,128)S(1)}, f32[36,12,128]{2,1,0:T(8,128)}, u32[]{:S(2)}) copy-start(f32[36,12,128]{2,1,0:T(8,128)} %get-tuple-element.15.hx_ref) | copy-start | bytes 663556
  14.8 0.8 %copy-start.16 = (f32[3,36,128]{2,1,0:T(8,128)S(1)}, f32[3,36,128]{2,1,0:T(8,128)}, u32[]{:S(2)}) copy-start(f32[3,36,128]{2,1,0:T(8,128)} %get-tuple-element.16.hy_ref) | copy-start | bytes 165892
  15.7 13.4 %copy-start.2 = (f32[3,2,3,3,3,12,128]{6,5,4,3,2,1,0:T(8,128)S(1)}, f32[3,2,3,3,3,12,128]{6,5,4,3,2,1,0:T(8,128)}, u32[]{:S(2)}) copy-start(f32[3,2,3,3,3,12,128]{6,5,4,3,2,1,0:T(8,128)} %copy-done) | copy-start | bytes 2985988
  19.6 0.7 %copy-start.3 = (f32[16,3,12,128]{3,2,1,0:T(8,128)}, f32[16,3,12,128]{3,2,1,0:T(8,128)S(1)}, u32[]{:S(2)}) copy-start(f32[16,3,12,128]{3,2,1,0:T(8,128)S(1)} %get-tuple-element.18.sx_ref.lx_ref) | copy-start | bytes 884740
  20.4 0.7 %copy-start.8 = (f32[16,3,13,128]{3,2,1,0:T(8,128)}, f32[16,3,13,128]{3,2,1,0:T(8,128)S(1)}, u32[]{:S(2)}) copy-start(f32[16,3,13,128]{3,2,1,0:T(8,128)S(1)} %get-tuple-element.19.ly_ref) | copy-start | bytes 958468
  21.1 0.6 copy-start.21
  29.1 1.0 %copy-start.4 = (f32[16,3,12,128]{3,2,1,0:T(8,128)S(1)}, f32[16,3,12,128]{3,2,1,0:T(8,128)}, u32[]{:S(2)}) copy-start(f32[16,3,12,128]{3,2,1,0:T(8,128)} %copy-done.3) | copy-start | bytes 884740
  30.1 1.0 %copy-start.9 = (f32[16,3,13,128]{3,2,1,0:T(8,128)S(1)}, f32[16,3,13,128]{3,2,1,0:T(8,128)}, u32[]{:S(2)}) copy-start(f32[16,3,13,128]{3,2,1,0:T(8,128)} %copy-done.8) | copy-start | bytes 958468
  31.1 0.9 %copy-start.13 = (f32[256,256]{1,0:T(8,128)S(1)}, f32[256,256]{1,0:T(8,128)}, u32[]{:S(2)}) copy-start(f32[256,256]{1,0:T(8,128)} %constant.14.clone.table_ref) | copy-start | bytes 786436
  32.1 0.9 %copy-start.15 = (f32[16,12,128]{2,1,0:T(8,128)S(1)}, f32[16,12,128]{2,1,0:T(8,128)}, u32[]{:S(2)}) copy-start(f32[16,12,128]{2,1,0:T(8,128)} %get-tuple-element.21.rx_ref) | copy-start | bytes 294916
  33.0 0.7 %copy-start.20 = (f32[3,16,128]{2,1,0:T(8,128)S(1)}, f32[3,16,128]{2,1,0:T(8,128)}, u32[]{:S(2)}) copy-start(f32[3,16,128]{2,1,0:T(8,128)} %get-tuple-element.22.ry_ref) | copy-start | bytes 73732
  33.7 14.0 %copy-start.11 = (f32[2,6,48,128]{3,2,1,0:T(8,128)S(1)}, f32[2,6,48,128]{3,2,1,0:T(8,128)}, u32[]{:S(2)}) copy-start(f32[2,6,48,128]{3,2,1,0:T(8,128)} %constant.20.clone.f_ref) | copy-start | bytes 884740
  35.5 0.7 %copy-start.14 = (f32[8,2,2,16,128]{4,3,2,1,0:T(8,128)}, f32[8,2,2,16,128]{4,3,2,1,0:T(8,128)S(1)}, u32[]{:S(2)}) copy-start(f32[8,2,2,16,128]{4,3,2,1,0:T(8,128)S(1)} %get-tuple-element.23) | copy-start | bytes 786436
  36.2 27.8 %copy-start.12 = (f32[256,256]{1,0:T(8,128)S(1)}, f32[256,256]{1,0:T(8,128)}, u32[]{:S(2)}) copy-start(f32[256,256]{1,0:T(8,128)} %constant.15.clone.table_ref) | copy-start | bytes 786436
  47.7 1.0 %copy-start.6 = (f32[16,2,16,128]{3,2,1,0:T(8,128)S(1)}, f32[16,2,16,128]{3,2,1,0:T(8,128)}, u32[]{:S(2)}) copy-start(f32[16,2,16,128]{3,2,1,0:T(8,128)} %shard_map.86.r_ref) | copy-start | bytes 786436
  48.7 0.8 %copy-start.17 = (f32[8,6,2,128]{3,2,1,0:T(2,128)S(1)}, f32[8,6,2,128]{3,2,1,0:T(2,128)}, u32[]{:S(2)}) copy-start(f32[8,6,2,128]{3,2,1,0:T(2,128)} %constant.19.clone.ci_ref) | copy-start | bytes 147460
  49.5 0.8 %copy-start.18 = (f32[6,8,2,128]{3,2,1,0:T(2,128)S(1)}, f32[6,8,2,128]{3,2,1,0:T(2,128)}, u32[]{:S(2)}) copy-start(f32[6,8,2,128]{3,2,1,0:T(2,128)} %constant.18.clone.cf_ref) | copy-start | bytes 147460
  50.3 0.8 %copy-start.19 = (f32[64,48]{1,0:T(8,128)S(1)}, f32[64,48]{1,0:T(8,128)}, u32[]{:S(2)}) copy-start(f32[64,48]{1,0:T(8,128)} %constant.17.clone.tyi_ref) | copy-start | bytes 36868
  51.0 0.7 %copy-start.22 = (f32[48,64]{1,0:T(8,128)S(1)}, f32[48,64]{1,0:T(8,128)}, u32[]{:S(2)}) copy-start(f32[48,64]{1,0:T(8,128)} %constant.16.clone.ty_ref) | copy-start | bytes 36868
  52.7 0.7 %copy-start.7 = (f32[16,2,16,128]{3,2,1,0:T(8,128)}, f32[16,2,16,128]{3,2,1,0:T(8,128)S(1)}, u32[]{:S(2)}) copy-start(f32[16,2,16,128]{3,2,1,0:T(8,128)S(1)} %shard_map.87.s_ref) | copy-start | bytes 786436
  64.0 1.0 %copy-start.5 = (f32[16,2,16,128]{3,2,1,0:T(8,128)S(1)}, f32[16,2,16,128]{3,2,1,0:T(8,128)}, u32[]{:S(2)}) copy-start(f32[16,2,16,128]{3,2,1,0:T(8,128)} %shard_map.88) | copy-start | bytes 786436
where the time goes:
time: 68.9 us; the launch traced here: 68.1 us
  Pallas kernels  47.9 us (70%)
  local copies, waits for them, and re-layouts  20 us (29%)
    pallas_call x2, Pallas kernels, swap(): pl.pallas_call(functools.partial(swap_kernel, sizes), out_shape=jax.Shape...  22 us
    unnamed x49, local copies, waits for them, and re-layouts  17.8 us
    pallas_call x2, Pallas kernels, exchange(): pl.pallas_call(functools.partial(exchange_kernel, sizes, way, pick), out_...  17.5 us
    pallas_call x4, Pallas kernels, local(): pl.pallas_call(kernel, out_shape=tuple((jax.ShapeDtypeStruct(s, jnp.float...  8.41 us
    reshape x1, local copies, waits for them, and re-layouts, shards(): return rotated.reshape(gauge_links.shape)  1.46 us

commit v1 on v0

--- a/solution.py
+++ b/solution.py
@@ -220,8 +220,14 @@
         target = n if n < 18 else n + 18
         for x in range(rows_x):
             ext[target, x, rows_y : rows_y + 1, :] = hy_ref[x, n : n + 1, :]
+    staple_planes(ext, gu_ref, lx_ref, ly_ref, rim_ref, lambda x: None)
+
+
+def staple_planes(ext, gu_ref, lx_ref, ly_ref, rim_ref, arrive):
+    rows_x, rows_y = gu_ref.shape[1], gu_ref.shape[2]
 
     def step(x, _):
+        arrive(x)
         for row in (0, rows_y - 8):
             here = slice(row, row + 8)
             acc = [None] * 3
@@ -256,7 +262,7 @@
                 for parts, shift, slot in ((low_i, j, 0), (low_j, i, 0 if j == 1 else 8)):
                     for n, p in enumerate(parts):
                         if shift == 0:
-                            lx_ref[slot + n, x, here, :] = p
+                            lx_ref[slot + n, x + 1, here, :] = p
                         elif shift == 1:
                             ly_ref[slot + n, x, row + 1 : row + 9, :] = p
                             if row:
@@ -270,16 +276,23 @@
 
 
 def smear_kernel(fast, l_ref, gu_ref, lx_ref, ly_ref, rx_ref, ry_ref, table_ref, v_ref, s_ref, a0, a1, dz, pack):
-    rows_x, rows_y = l_ref.shape[1], l_ref.shape[2]
-
-    def step(x, _):
-        before = jnp.maximum(x - 1, 0)
+    smear_sites(fast, l_ref, gu_ref, lx_ref, ly_ref, rx_ref, ry_ref, table_ref, v_ref, s_ref, a0, a1, dz, pack, lambda x: None)
+
+
+def smear_sites(fast, l_ref, gu_ref, lx_ref, ly_ref, rx_ref, ry_ref, table_ref, v_ref, s_ref, a0, a1, dz, pack, arrive):
+    rows_x, rows_y = v_ref.shape[1], v_ref.shape[2]
+
+    def step(n_step, _):
+        x = rows_x - 1 - n_step
+        arrive(x)
         for row in (0, rows_y - 8):
             here = slice(row, row + 8)
             top = lax.broadcasted_iota(jnp.int32, (8, 128), 0) == 0
 
             def low_x(n):
-                return jnp.where(x == 0, rx_ref[n, here, :], lx_ref[n, before, here, :])
+                if rx_ref is None:
+                    return lx_ref[n, x, here, :]
+                return jnp.where(x == 0, rx_ref[n, here, :], lx_ref[n, x, here, :])
 
             def low_y(n):
                 value = ly_ref[n, x, here, :]
@@ -352,7 +365,7 @@
     for m in range(6):
         total = None
         for n in range(8):
-            term = planes[n] * cf_ref[m, n, 0:1, :] + turned[n] * cf_ref[m, n, 1:2, :]
+            term = planes[n] * cf_ref[m, 2 * n : 2 * n + 1, :] + turned[n] * cf_ref[m, 2 * n + 1 : 2 * n + 2, :]
             total = term if total is None else total + term
         modes.append(total * f_ref[half, m])
     turned = [pltpu.roll(p, 64, 1) for p in modes]
@@ -360,13 +373,13 @@
         for xp in range(2):
             total = None
             for m in range(6):
-                term = modes[m] * ci_ref[2 * gx + xp, m, 0:1, :] + turned[m] * ci_ref[2 * gx + xp, m, 1:2, :]
+                term = modes[m] * ci_ref[2 * gx + xp, 2 * m : 2 * m + 1, :] + turned[m] * ci_ref[2 * gx + xp, 2 * m + 1 : 2 * m + 2, :]
                 total = term if total is None else total + term
             out = jnp.dot(tyi_ref[...], total, precision=HIGHEST, preferred_element_type=jnp.float32)
             o_ref[4 * gx : 4 * gx + 4, xp] = out.reshape(4, 16, 128)
 
 
-def rotate_kernel(fast, q_ref, v_ref, table_ref, o_ref, acc, g):
+def rotate_kernel(fast, q_ref, v_ref, table_ref, o_ref, acc, g, woven=False):
     rows_x, rows_y = v_ref.shape[1], v_ref.shape[2]
     if fast:
         left = jnp.concatenate([q_ref[:, 0].reshape(256, 128), q_ref[:, 1].reshape(256, 128)], axis=1)
@@ -404,7 +417,11 @@
                 for r in range(3):
                     for c in range(3):
                         for part in range(2):
-                            o_ref[18 * direction + 9 * part + 3 * r + c, x, here, :] = out[r][c][part]
+                            if woven:
+                                rows = pl.ds(2 * row + part, 8, stride=2)
+                                o_ref[9 * direction + 3 * r + c, x, rows, :] = out[r][c][part]
+                            else:
+                                o_ref[18 * direction + 9 * part + 3 * r + c, x, here, :] = out[r][c][part]
         return 0
 
     lax.fori_loop(0, rows_x, step, 0)
@@ -461,61 +478,6 @@
         scratch_shapes=[pltpu.SemaphoreType.DMA((2,)), pltpu.SemaphoreType.DMA((2,))],
         compiler_params=pltpu.CompilerParams(collective_id=key, has_side_effects=True),
     )(sx, sy)
-
-
-def swap_kernel(sizes, s_ref, r_ref, send, recv, local):
-    n_x, n_y, n_z = sizes
-    total = n_x * n_y * n_z
-    me = (lax.axis_index("gx") * n_y + lax.axis_index("gy")) * n_z + lax.axis_index("gz")
-
-    def device(index):
-        return {
-            "gx": lax.div(index, n_y * n_z),
-            "gy": lax.rem(lax.div(index, n_z), n_y),
-            "gz": lax.rem(index, n_z),
-        }
-
-    barrier = pltpu.get_barrier_semaphore()
-    for offset in range(1, total):
-        pl.semaphore_signal(
-            barrier, inc=1, device_id=device(lax.rem(me + offset, total)), device_id_type=MESH
-        )
-    own = pltpu.make_async_copy(s_ref.at[me], r_ref.at[me], local)
-    own.start()
-    pl.semaphore_wait(barrier, total - 1)
-    copies = []
-    for offset in sorted(range(1, total), key=lambda o: -min(o, total - o)):
-        peer = lax.rem(me + offset, total)
-        copies.append(
-            pltpu.make_async_remote_copy(
-                src_ref=s_ref.at[peer],
-                dst_ref=r_ref.at[me],
-                send_sem=send.at[offset],
-                recv_sem=recv.at[offset],
-                device_id=device(peer),
-                device_id_type=MESH,
-            )
-        )
-        copies[-1].start()
-    own.wait()
-    for copy in copies:
-        copy.wait()
-
-
-def swap(sizes, key, blocks):
-    total = blocks.shape[0]
-    return pl.pallas_call(
-        functools.partial(swap_kernel, sizes),
-        out_shape=jax.ShapeDtypeStruct(blocks.shape, jnp.float32),
-        in_specs=[ANY],
-        out_specs=ANY,
-        scratch_shapes=[
-            pltpu.SemaphoreType.DMA((total,)),
-            pltpu.SemaphoreType.DMA((total,)),
-            pltpu.SemaphoreType.DMA,
-        ],
-        compiler_params=pltpu.CompilerParams(collective_id=key, has_side_effects=True),
-    )(blocks)
 
 
 def real_basis(length):
@@ -571,8 +533,8 @@
         flat(wide.T.copy(), (256, 256)),
         flat(fy, (48, 64)),
         flat(iy, (64, 48)),
-        flat(cf, (6, 8, 2, 128)),
-        flat(ci, (8, 6, 2, 128)),
+        flat(cf, (6, 16, 128)),
+        flat(ci, (8, 12, 128)),
         flat(factor, (2, 6, 48, 128)),
     )
 
@@ -590,10 +552,181 @@
     return out[0] if single else out
 
 
+def fused_kernel(sizes, *refs):
+    l_ref, tables_hbm, o_ref = refs[0], refs[1:8], refs[8]
+    tables_ref = refs[9:16]
+    lv, hx, edge, hy, ext, gu, lx, ly, rim, ry, v, a0, a1, dz, pack, s, r, s2, q, acc, g = refs[16:37]
+    send, recv, near = refs[37:]
+    wide, wide_back, fy, iy, cf, ci, factor = tables_ref
+    n_x, n_y, n_z = sizes
+    total = n_x * n_y * n_z
+    rows_x, rows_y = v.shape[1], v.shape[2]
+    me = (lax.axis_index("gx") * n_y + lax.axis_index("gy")) * n_z + lax.axis_index("gz")
+
+    def device(index):
+        return {
+            "gx": lax.div(index, n_y * n_z),
+            "gy": lax.rem(lax.div(index, n_z), n_y),
+            "gz": lax.rem(index, n_z),
+        }
+
+    pulls = [pltpu.make_async_copy(l_ref, lv, near.at[7])]
+    pulls += [pltpu.make_async_copy(tables_hbm[n], tables_ref[n], near.at[n]) for n in range(7)]
+    for pull in pulls:
+        pull.start()
+    barrier = pltpu.get_barrier_semaphore()
+    for offset in range(1, total):
+        pl.semaphore_signal(
+            barrier, inc=1, device_id=device(lax.rem(me + offset, total)), device_id_type=MESH
+        )
+    started = []
+
+    def push(slot, src, dst, target):
+        copy = pltpu.make_async_remote_copy(
+            src_ref=src,
+            dst_ref=dst,
+            send_sem=send.at[slot],
+            recv_sem=recv.at[slot],
+            device_id=target,
+            device_id_type=MESH,
+        )
+        copy.start()
+        started.append(copy)
+        return copy
+
+    pl.semaphore_wait(barrier, total - 1)
+    face = push(0, l_ref.at[pl.ds(9, 18), 0], hx, neighbour(sizes, -1, 0))
+    pulls[0].wait()
+    for d in range(3):
+
+        def fill(n, _):
+            for part in range(2):
+                ext[18 * d + 9 * part + n, 0:rows_x, 0:rows_y, :] = lv[
+                    9 * d + n, :, pl.ds(part, rows_y, stride=2), :
+                ]
+            return 0
+
+        if d == 1:
+            continue
+        lax.fori_loop(0, 9, fill, 0)
+    for n in range(36):
+        source = n if n < 18 else n + 18
+        for x in range(rows_x):
+            edge[x, n : n + 1, :] = ext[source, x, 0:1, :]
+    line = push(1, edge, hy, neighbour(sizes, 0, -1))
+
+    def fill_middle(n, _):
+        for part in range(2):
+            ext[18 + 9 * part + n, 0:rows_x, 0:rows_y, :] = lv[9 + n, :, pl.ds(part, rows_y, stride=2), :]
+        return 0
+
+    lax.fori_loop(0, 9, fill_middle, 0)
+    line.wait_recv()
+    for n in range(36):
+        target = n if n < 18 else n + 18
+        for x in range(rows_x):
+            ext[target, x, rows_y : rows_y + 1, :] = hy[x, n : n + 1, :]
+
+    def face_arrives(x):
+        @pl.when(x == rows_x - 1)
+        def _():
+            face.wait_recv()
+
+            def fill_face(n, _):
+                for d in range(2):
+                    for part in range(2):
+                        ext[18 * d + 18 + 9 * part + n, rows_x, 0:rows_y, :] = hx[
+                            9 * d + n, pl.ds(part, rows_y, stride=2), :
+                        ]
+                return 0
+
+            lax.fori_loop(0, 9, fill_face, 0)
+
+    staple_planes(ext, gu, lx, ly, rim, face_arrives)
+    low_line = push(3, rim, ry, neighbour(sizes, 0, 1))
+    low_face = push(2, lx.at[:, rows_x], lx.at[:, 0], neighbour(sizes, 1, 0))
+    pulls[1].wait()
+    low_line.wait_recv()
+
+    def low_face_arrives(x):
+        @pl.when(x == 0)
+        def _():
+            low_face.wait_recv()
+
+    smear_sites(True, ext, gu, lx, ly, None, ry, wide, v, s, a0, a1, dz, pack, low_face_arrives)
+    order = sorted(range(1, total), key=lambda o: -min(o, total - o))
+    copies = []
+    for offset in order:
+        peer = lax.rem(me + offset, total)
+        copies.append(push(3 + offset, s.at[lax.div(peer, 2), lax.rem(peer, 2)], r.at[me], device(peer)))
+    r[me] = s[lax.div(me, 2), lax.rem(me, 2)]
+    for pull in pulls[2:]:
+        pull.wait()
+    for copy in copies:
+        copy.wait_recv()
+    solve_kernel(r, fy, iy, cf, ci, factor, s2)
+    copies = []
+    for offset in order:
+        peer = lax.rem(me + offset, total)
+        copies.append(push(18 + offset, s2.at[peer], q.at[lax.div(me, 2), lax.rem(me, 2)], device(peer)))
+    q[lax.div(me, 2), lax.rem(me, 2)] = s2[me]
+    for copy in copies:
+        copy.wait_recv()
+    rotate_kernel(True, q, v, wide_back, o_ref, acc, g, woven=True)
+    for copy in started:
+        copy.wait_send()
+
+
+def fused(sizes, gauge_links):
+    rows_x, rows_y, depth = gauge_links.shape[4:]
+    woven = jnp.transpose(gauge_links, (0, 2, 3, 4, 5, 1, 6)).reshape(27, rows_x, 2 * rows_y, depth)
+    given = tables()
+    shapes = [t.shape for t in given] + [
+        woven.shape,
+        (18, 2 * rows_y, depth),
+        (rows_x, 36, depth),
+        (rows_x, 36, depth),
+        (54, rows_x + 1, 16, depth),
+        (24, rows_x, rows_y, depth),
+        (16, rows_x + 1, rows_y, depth),
+        (16, rows_x, rows_y + 1, depth),
+        (rows_x, 16, depth),
+        (rows_x, 16, depth),
+        (54, rows_x, rows_y, depth),
+        (8, rows_x, rows_y, depth),
+        (8, rows_x, rows_y + 1, depth),
+        (8, rows_x, rows_y, depth),
+        (8, 2, 16, 256),
+        (8, 2, 2, 16, 128),
+        (16, 2, 16, 128),
+        (16, 2, 16, 128),
+        (8, 2, 2, 16, 128),
+        (8, 4, 16, 128),
+        (18, rows_x + 1, 16, depth),
+    ]
+    out = pl.pallas_call(
+        functools.partial(fused_kernel, sizes),
+        out_shape=jax.ShapeDtypeStruct(woven.shape, jnp.float32),
+        in_specs=[pl.BlockSpec(memory_space=pltpu.HBM)] * 8,
+        out_specs=VMEM,
+        scratch_shapes=[pltpu.VMEM(shape, jnp.float32) for shape in shapes]
+        + [
+            pltpu.SemaphoreType.DMA((34,)),
+            pltpu.SemaphoreType.DMA((34,)),
+            pltpu.SemaphoreType.DMA((8,)),
+        ],
+        compiler_params=pltpu.CompilerParams(
+            collective_id=5, has_side_effects=True, vmem_limit_bytes=(64 << 20) - (1 << 19)
+        ),
+    )(woven, *given)
+    return jnp.transpose(out.reshape(3, 3, 3, rows_x, rows_y, 2, depth), (0, 5, 1, 2, 3, 4, 6))
+
+
 def shards(sizes, gauge_links):
+    if sizes == (4, 2, 2):
+        return fused(sizes, gauge_links)
     rows_x, rows_y, depth = gauge_links.shape[4:]
-    fast = sizes == (4, 2, 2)
-    wide, wide_back, fy, iy, cf, ci, factor = tables()
+    wide, wide_back = tables()[:2]
     links = gauge_links.reshape(54, rows_x, rows_y, depth)
     first = links[:, :, 0, :]
     edge = jnp.moveaxis(jnp.concatenate([first[:18], first[36:]], axis=0), 0, 1)
@@ -602,7 +735,7 @@
         staple_kernel,
         (
             (24, rows_x, rows_y, depth),
-            (16, rows_x, rows_y, depth),
+            (16, rows_x + 1, rows_y, depth),
             (16, rows_x, rows_y + 1, depth),
             (rows_x, 16, depth),
         ),
@@ -611,11 +744,10 @@
         hx,
         hy,
     )
-    rx, ry = exchange(sizes, 1, (0, 16, rows_x - 1), 2, lx, rim)
-    spectral = (8, 2, 2, 16, 128) if fast else (8, 2, 16, 256)
+    rx, ry = exchange(sizes, 1, (0, 16, rows_x), 2, lx, rim)
     smeared, blocks = local(
-        functools.partial(smear_kernel, fast),
-        ((54, rows_x, rows_y, depth), spectral),
+        functools.partial(smear_kernel, False),
+        ((54, rows_x, rows_y, depth), (8, 2, 16, 256)),
         [
             (8, rows_x, rows_y, depth),
             (8, rows_x, rows_y + 1, depth),
@@ -630,17 +762,12 @@
         ry,
         wide,
     )
-    if fast:
-        received = swap(sizes, 3, blocks.reshape(16, 2, 16, 128))
-        solved = local(solve_kernel, (16, 2, 16, 128), [], received, fy, iy, cf, ci, factor)
-        accel = swap(sizes, 4, solved).reshape(8, 2, 2, 16, 128)
-    else:
-        used = blocks[:, :, : rows_y + 1]
-        payload = jnp.concatenate([used[..., :depth], used[..., depth:]], axis=1)
-        accel = general_solve(payload, rows_x, rows_y, depth)
-        accel = jnp.pad(accel, ((0, 0), (0, 0), (0, 16 - accel.shape[2]), (0, 0)))
+    used = blocks[:, :, : rows_y + 1]
+    payload = jnp.concatenate([used[..., :depth], used[..., depth:]], axis=1)
+    accel = general_solve(payload, rows_x, rows_y, depth)
+    accel = jnp.pad(accel, ((0, 0), (0, 0), (0, 16 - accel.shape[2]), (0, 0)))
     rotated = local(
-        functools.partial(rotate_kernel, fast),
+        functools.partial(rotate_kernel, False),
         (54, rows_x, rows_y, depth),
         [(8, 4, 16, 128), (18, rows_x + 1, 16, depth)],
         accel,

time: 68.9 us -> 41.1 us (0.60)
  local copies, waits for them, and re-layouts: 20 us -> 2.22 us
  Pallas kernels: 47.9 us -> 38.8 us
    unnamed x49 -> x1, local copies, waits for them, and re-layouts: 17.8 us -> 2.22 us
    pallas_call x8 -> x1, Pallas kernels: 47.9 us -> 38.8 us  [fused(): pl.pallas_call(functools.partial(fused_kernel, sizes), out_shape=jax.Shap...]
    reshape x1 -> x0, local copies, waits for them, and re-layouts: 1.46 us -> none  [shards(): return rotated.reshape(gauge_links.shape)]
    transpose x1 -> x0, local copies, waits for them, and re-layouts: 0.78 us -> none  [shards(): edge = jnp.moveaxis(jnp.concatenate([first[:18], first[36:]], axis=0), 0, 1)]
where the time goes in v1:
time: 41.1 us; the launch traced here: 41 us
  Pallas kernels  38.8 us (94%)
  local copies, waits for them, and re-layouts  2.22 us (5%)
    pallas_call x1, Pallas kernels, fused(): pl.pallas_call(functools.partial(fused_kernel, sizes), out_shape=jax.Shap...  38.8 us
    unnamed x1, local copies, waits for them, and re-layouts  2.22 us

profile of v1, /device:TPU:0, one launch (start us, length us, event | category | flops | bytes accessed | tf_op | source)
XLA Modules:
  0.0 41.0 jit_solution(11573621324633502031)
XLA Ops:
  0.0 38.8 %shard_map.82 = f32[27,3,24,128]{3,2,1,0:T(8,128)} custom-call(f32[27,3,24,128]{3,2,1,0:T(8,128)} %bitcast.7, f32[256,256]{1,0:T(8,128)} %constant.14.clone.refs_1_, f32[256,256]{1,0:T(8,128)} %constant.15.clone.refs_2_, f32[48,64]{1,0:T(8,128)} %constant.16.clone.refs_3_, f32[64,48]{1,0:T(8,128)} %constant.17.clone.refs_4_, ...), custom_call_target="tpu_custom_call" | custom-call | tf_op jit(solution)/shard_map/pallas_call | solution.py:707
  38.8 2.2 %copy.10 = f32[3,2,3,3,3,12,128]{6,1,5,4,3,2,0:T(2,128)} copy(f32[3,2,3,3,3,12,128]{6,1,5,4,3,2,0:T(2,128)} %bitcast.6) | data formatting | bytes 1990656

commit v2 on v1

--- a/solution.py
+++ b/solution.py
@@ -351,32 +351,38 @@
         s_ref[...] = pack[...]
 
 
-def solve_kernel(r_ref, ty_ref, tyi_ref, cf_ref, ci_ref, f_ref, o_ref):
+def solve_blocks(r_ref, ty_ref, tyi_ref, cf_ref, ci_ref, f_ref, o_ref, ready, done):
     half = lax.axis_index("gz")
-    planes = []
-    for gx in range(4):
+    mine = lax.axis_index("gx")
+    modes = [None] * 6
+    for k in (0, 1, 3, 2):
+        ready(k)
+        gx = lax.rem(mine + 4 - k, 4)
         for xp in range(2):
-            block = r_ref[4 * gx : 4 * gx + 4, xp].reshape(64, 128)
-            planes.append(
-                jnp.dot(ty_ref[...], block, precision=HIGHEST, preferred_element_type=jnp.float32)
-            )
-    turned = [pltpu.roll(p, 64, 1) for p in planes]
-    modes = []
-    for m in range(6):
-        total = None
-        for n in range(8):
-            term = planes[n] * cf_ref[m, 2 * n : 2 * n + 1, :] + turned[n] * cf_ref[m, 2 * n + 1 : 2 * n + 2, :]
-            total = term if total is None else total + term
-        modes.append(total * f_ref[half, m])
+            block = r_ref[pl.ds(4 * gx, 4), xp].reshape(64, 128)
+            plane = jnp.dot(ty_ref[...], block, precision=HIGHEST, preferred_element_type=jnp.float32)
+            turned = pltpu.roll(plane, 64, 1)
+            for m in range(6):
+                term = (
+                    plane * cf_ref[2 * gx + xp, 2 * m : 2 * m + 1, :]
+                    + turned * cf_ref[2 * gx + xp, 2 * m + 1 : 2 * m + 2, :]
+                )
+                modes[m] = term if modes[m] is None else modes[m] + term
+    modes = [modes[m] * f_ref[half, m] for m in range(6)]
     turned = [pltpu.roll(p, 64, 1) for p in modes]
-    for gx in range(4):
+    for k in (2, 1, 3, 0):
+        gx = lax.rem(mine + k, 4)
         for xp in range(2):
             total = None
             for m in range(6):
-                term = modes[m] * ci_ref[2 * gx + xp, 2 * m : 2 * m + 1, :] + turned[m] * ci_ref[2 * gx + xp, 2 * m + 1 : 2 * m + 2, :]
+                term = (
+                    modes[m] * ci_ref[2 * gx + xp, 2 * m : 2 * m + 1, :]
+                    + turned[m] * ci_ref[2 * gx + xp, 2 * m + 1 : 2 * m + 2, :]
+                )
                 total = term if total is None else total + term
             out = jnp.dot(tyi_ref[...], total, precision=HIGHEST, preferred_element_type=jnp.float32)
-            o_ref[4 * gx : 4 * gx + 4, xp] = out.reshape(4, 16, 128)
+            o_ref[pl.ds(4 * gx, 4), xp] = out.reshape(4, 16, 128)
+        done(k)
 
 
 def rotate_kernel(fast, q_ref, v_ref, table_ref, o_ref, acc, g, woven=False):
@@ -511,7 +517,7 @@
         fy[:, b, 12] = -ty[:, (12 * b + 12) % 48]
         for r in range(13):
             iy[b, r] = ty[:, (12 * b + r) % 48]
-    cf = np.zeros((6, 8, 2, 2, 64))
+    cf = np.zeros((8, 6, 2, 2, 64))
     ci = np.zeros((8, 6, 2, 2, 64))
     factor = np.zeros((2, 6, 48, 2, 64))
     for m in range(6):
@@ -524,7 +530,7 @@
                         x = xp + 2 * (q if turn == 0 else 1 - q)
                         kx = m + 6 * q
                         site = (3 * gx + x) % 12
-                        cf[m, 2 * gx + xp, turn, q] = -tx[kx, site] if x == 3 else tx[kx, site]
+                        cf[2 * gx + xp, m, turn, q] = -tx[kx, site] if x == 3 else tx[kx, site]
                         back = m + 6 * (q if turn == 0 else 1 - q)
                         ci[2 * gx + xp, m, turn, q] = tx[back, (3 * gx + xp + 2 * q) % 12]
     flat = lambda t, shape: jnp.asarray(t.reshape(shape), jnp.float32)
@@ -533,7 +539,7 @@
         flat(wide.T.copy(), (256, 256)),
         flat(fy, (48, 64)),
         flat(iy, (64, 48)),
-        flat(cf, (6, 16, 128)),
+        flat(cf, (8, 12, 128)),
         flat(ci, (8, 12, 128)),
         flat(factor, (2, 6, 48, 128)),
     )
@@ -574,6 +580,7 @@
     pulls += [pltpu.make_async_copy(tables_hbm[n], tables_ref[n], near.at[n]) for n in range(7)]
     for pull in pulls:
         pull.start()
+    r[...] = jnp.zeros(r.shape, jnp.float32)
     barrier = pltpu.get_barrier_semaphore()
     for offset in range(1, total):
         pl.semaphore_signal(
@@ -654,23 +661,46 @@
             low_face.wait_recv()
 
     smear_sites(True, ext, gu, lx, ly, None, ry, wide, v, s, a0, a1, dz, pack, low_face_arrives)
-    order = sorted(range(1, total), key=lambda o: -min(o, total - o))
-    copies = []
-    for offset in order:
-        peer = lax.rem(me + offset, total)
-        copies.append(push(3 + offset, s.at[lax.div(peer, 2), lax.rem(peer, 2)], r.at[me], device(peer)))
-    r[me] = s[lax.div(me, 2), lax.rem(me, 2)]
+    used = rows_y + 1
+    mine, spot = lax.div(me, 4), lax.rem(me, 4)
+    there, back = {}, {}
+
+    def partner(k, j):
+        return 4 * lax.rem(mine + k, 4) + lax.rem(spot + j, 4)
+
+    for k in (2, 1, 3, 0):
+        for j in range(4):
+            if k or j:
+                peer = partner(k, j)
+                there[k, j] = push(
+                    3 + 4 * k + j,
+                    s.at[lax.div(peer, 2), lax.rem(peer, 2), :, pl.ds(0, used)],
+                    r.at[me, :, pl.ds(0, used)],
+                    device(peer),
+                )
+    r[me, :, 0:used, :] = s[lax.div(me, 2), lax.rem(me, 2), :, 0:used, :]
     for pull in pulls[2:]:
         pull.wait()
-    for copy in copies:
-        copy.wait_recv()
-    solve_kernel(r, fy, iy, cf, ci, factor, s2)
-    copies = []
-    for offset in order:
-        peer = lax.rem(me + offset, total)
-        copies.append(push(18 + offset, s2.at[peer], q.at[lax.div(me, 2), lax.rem(me, 2)], device(peer)))
-    q[lax.div(me, 2), lax.rem(me, 2)] = s2[me]
-    for copy in copies:
+
+    def ready(k):
+        for j in range(4):
+            if k or j:
+                there[k, j].wait_recv()
+
+    def done(k):
+        for j in range(4):
+            if k or j:
+                peer = partner(k, j)
+                back[k, j] = push(
+                    18 + 4 * k + j,
+                    s2.at[peer, :, pl.ds(0, used)],
+                    q.at[lax.div(me, 2), lax.rem(me, 2), :, pl.ds(0, used)],
+                    device(peer),
+                )
+
+    solve_blocks(r, fy, iy, cf, ci, factor, s2, ready, done)
+    q[lax.div(me, 2), lax.rem(me, 2), :, 0:used, :] = s2[me, :, 0:used, :]
+    for copy in back.values():
         copy.wait_recv()
     rotate_kernel(True, q, v, wide_back, o_ref, acc, g, woven=True)
     for copy in started:

time: 41.1 us -> 38.8 us (0.944)
  Pallas kernels: 38.8 us -> 36.4 us
    pallas_call x1, Pallas kernels: 38.8 us -> 36.4 us  [fused(): pl.pallas_call(functools.partial(fused_kernel, sizes), out_shape=jax.Shap...]
where the time goes in v2:
time: 38.8 us; the launch traced here: 38.6 us
  Pallas kernels  36.4 us (94%)
  local copies, waits for them, and re-layouts  2.22 us (6%)
    pallas_call x1, Pallas kernels, fused(): pl.pallas_call(functools.partial(fused_kernel, sizes), out_shape=jax.Shap...  36.4 us
    unnamed x1, local copies, waits for them, and re-layouts  2.22 us

profile of v2, /device:TPU:0, one launch (start us, length us, event | category | flops | bytes accessed | tf_op | source)
XLA Modules:
  0.0 38.6 jit_solution(9955704598010544527)
XLA Ops:
  0.0 36.4 %shard_map.82 = f32[27,3,24,128]{3,2,1,0:T(8,128)} custom-call(f32[27,3,24,128]{3,2,1,0:T(8,128)} %bitcast.7, f32[256,256]{1,0:T(8,128)} %constant.14.clone.refs_1_, f32[256,256]{1,0:T(8,128)} %constant.15.clone.refs_2_, f32[48,64]{1,0:T(8,128)} %constant.16.clone.refs_3_, f32[64,48]{1,0:T(8,128)} %constant.17.clone.refs_4_, ...), custom_call_target="tpu_custom_call" | custom-call | tf_op jit(solution)/shard_map/pallas_call | solution.py:737
  36.4 2.2 %copy.10 = f32[3,2,3,3,3,12,128]{6,1,5,4,3,2,0:T(2,128)} copy(f32[3,2,3,3,3,12,128]{6,1,5,4,3,2,0:T(2,128)} %bitcast.6) | data formatting | bytes 1990656

commit v3 on v2

--- a/solution.py
+++ b/solution.py
@@ -385,7 +385,7 @@
         done(k)
 
 
-def rotate_kernel(fast, q_ref, v_ref, table_ref, o_ref, acc, g, woven=False):
+def rotate_kernel(fast, q_ref, v_ref, table_ref, o_ref, acc, g, woven=False, finish=None):
     rows_x, rows_y = v_ref.shape[1], v_ref.shape[2]
     if fast:
         left = jnp.concatenate([q_ref[:, 0].reshape(256, 128), q_ref[:, 1].reshape(256, 128)], axis=1)
@@ -428,6 +428,8 @@
                                 o_ref[9 * direction + 3 * r + c, x, rows, :] = out[r][c][part]
                             else:
                                 o_ref[18 * direction + 9 * part + 3 * r + c, x, here, :] = out[r][c][part]
+        if finish is not None:
+            finish(x)
         return 0
 
     lax.fori_loop(0, rows_x, step, 0)
@@ -561,8 +563,8 @@
 def fused_kernel(sizes, *refs):
     l_ref, tables_hbm, o_ref = refs[0], refs[1:8], refs[8]
     tables_ref = refs[9:16]
-    lv, hx, edge, hy, ext, gu, lx, ly, rim, ry, v, a0, a1, dz, pack, s, r, s2, q, acc, g = refs[16:37]
-    send, recv, near = refs[37:]
+    lv, hx, edge, hy, ext, gu, lx, ly, rim, ry, v, a0, a1, dz, pack, s, r, s2, q, acc, g, planes = refs[16:38]
+    send, recv, near, out_sem = refs[38:]
     wide, wide_back, fy, iy, cf, ci, factor = tables_ref
     n_x, n_y, n_z = sizes
     total = n_x * n_y * n_z
@@ -702,7 +704,13 @@
     q[lax.div(me, 2), lax.rem(me, 2), :, 0:used, :] = s2[me, :, 0:used, :]
     for copy in back.values():
         copy.wait_recv()
-    rotate_kernel(True, q, v, wide_back, o_ref, acc, g, woven=True)
+
+    def store(x):
+        return pltpu.make_async_copy(planes.at[:, x], o_ref.at[:, x], out_sem.at[x])
+
+    rotate_kernel(True, q, v, wide_back, planes, acc, g, woven=True, finish=lambda x: store(x).start())
+    for x in range(rows_x):
+        store(x).wait()
     for copy in started:
         copy.wait_send()
 
@@ -733,17 +741,19 @@
         (8, 2, 2, 16, 128),
         (8, 4, 16, 128),
         (18, rows_x + 1, 16, depth),
+        woven.shape,
     ]
     out = pl.pallas_call(
         functools.partial(fused_kernel, sizes),
         out_shape=jax.ShapeDtypeStruct(woven.shape, jnp.float32),
         in_specs=[pl.BlockSpec(memory_space=pltpu.HBM)] * 8,
-        out_specs=VMEM,
+        out_specs=pl.BlockSpec(memory_space=pltpu.HBM),
         scratch_shapes=[pltpu.VMEM(shape, jnp.float32) for shape in shapes]
         + [
             pltpu.SemaphoreType.DMA((34,)),
             pltpu.SemaphoreType.DMA((34,)),
             pltpu.SemaphoreType.DMA((8,)),
+            pltpu.SemaphoreType.DMA((rows_x,)),
         ],
         compiler_params=pltpu.CompilerParams(
             collective_id=5, has_side_effects=True, vmem_limit_bytes=(64 << 20) - (1 << 19)

time: 38.8 us -> 38.6 us (level)
  no operation moved by 1% of the time
where the time goes in v3:
time: 38.6 us; the launch traced here: 38.4 us
  Pallas kernels  36.2 us (94%)
  local copies, waits for them, and re-layouts  2.22 us (6%)
    pallas_call x1, Pallas kernels, fused(): pl.pallas_call(functools.partial(fused_kernel, sizes), out_shape=jax.Shap...  36.2 us
    unnamed x1, local copies, waits for them, and re-layouts  2.22 us

profile of v3, /device:TPU:0, one launch (start us, length us, event | category | flops | bytes accessed | tf_op | source)
XLA Modules:
  0.0 38.4 jit_solution(13440744642588749872)
XLA Ops:
  0.0 36.2 %shard_map.82 = f32[27,3,24,128]{3,2,1,0:T(8,128)} custom-call(f32[27,3,24,128]{3,2,1,0:T(8,128)} %bitcast.7, f32[256,256]{1,0:T(8,128)} %constant.14.clone.refs_1_, f32[256,256]{1,0:T(8,128)} %constant.15.clone.refs_2_, f32[48,64]{1,0:T(8,128)} %constant.16.clone.refs_3_, f32[64,48]{1,0:T(8,128)} %constant.17.clone.refs_4_, ...), custom_call_target="tpu_custom_call" | custom-call | tf_op jit(solution)/shard_map/pallas_call | solution.py:746
  36.2 2.2 %copy.10 = f32[3,2,3,3,3,12,128]{6,1,5,4,3,2,0:T(2,128)} copy(f32[3,2,3,3,3,12,128]{6,1,5,4,3,2,0:T(2,128)} %bitcast.6) | data formatting | bytes 1990656

commit v4 on v3

--- a/solution.py
+++ b/solution.py
@@ -604,7 +604,10 @@
         return copy
 
     pl.semaphore_wait(barrier, total - 1)
-    face = push(0, l_ref.at[pl.ds(9, 18), 0], hx, neighbour(sizes, -1, 0))
+    faces = [
+        push(slot, l_ref.at[pl.ds(9 + first, 9), 0], hx.at[pl.ds(first, 9)], neighbour(sizes, -1, 0))
+        for slot, first in ((0, 0), (34, 9))
+    ]
     pulls[0].wait()
     for d in range(3):
 
@@ -639,7 +642,8 @@
     def face_arrives(x):
         @pl.when(x == rows_x - 1)
         def _():
-            face.wait_recv()
+            for face in faces:
+                face.wait_recv()
 
             def fill_face(n, _):
                 for d in range(2):
@@ -750,8 +754,8 @@
         out_specs=pl.BlockSpec(memory_space=pltpu.HBM),
         scratch_shapes=[pltpu.VMEM(shape, jnp.float32) for shape in shapes]
         + [
-            pltpu.SemaphoreType.DMA((34,)),
-            pltpu.SemaphoreType.DMA((34,)),
+            pltpu.SemaphoreType.DMA((35,)),
+            pltpu.SemaphoreType.DMA((35,)),
             pltpu.SemaphoreType.DMA((8,)),
             pltpu.SemaphoreType.DMA((rows_x,)),
         ],

time: 38.6 us -> 38.6 us (level)
  no operation moved by 1% of the time
where the time goes in v4:
time: 38.6 us; the launch traced here: 38.4 us
  Pallas kernels  36.2 us (94%)
  local copies, waits for them, and re-layouts  2.22 us (6%)
    pallas_call x1, Pallas kernels, fused(): pl.pallas_call(functools.partial(fused_kernel, sizes), out_shape=jax.Shap...  36.2 us
    unnamed x1, local copies, waits for them, and re-layouts  2.22 us

profile of v4, /device:TPU:0, one launch (start us, length us, event | category | flops | bytes accessed | tf_op | source)
XLA Modules:
  0.0 38.4 jit_solution(8629330933353207743)
XLA Ops:
  0.0 36.2 %shard_map.82 = f32[27,3,24,128]{3,2,1,0:T(8,128)} custom-call(f32[27,3,24,128]{3,2,1,0:T(8,128)} %bitcast.7, f32[256,256]{1,0:T(8,128)} %constant.14.clone.refs_1_, f32[256,256]{1,0:T(8,128)} %constant.15.clone.refs_2_, f32[48,64]{1,0:T(8,128)} %constant.16.clone.refs_3_, f32[64,48]{1,0:T(8,128)} %constant.17.clone.refs_4_, ...), custom_call_target="tpu_custom_call" | custom-call | tf_op jit(solution)/shard_map/pallas_call | solution.py:750
  36.2 2.2 %copy.10 = f32[3,2,3,3,3,12,128]{6,1,5,4,3,2,0:T(2,128)} copy(f32[3,2,3,3,3,12,128]{6,1,5,4,3,2,0:T(2,128)} %bitcast.6) | data formatting | bytes 1990656
